TPU v7x, 32 devices: a whole 2x2x4 slice. The times are simulated.
32 devices in a mesh: batch: 8 (over z, core), head: 4 (over y, x).
Axes of the slice: x: 2, y: 2, z: 4, core: 2. Of those that a mesh axis runs over, the one named last changes fastest.
Arguments:
- hidden_in: bfloat16 [2048, 2048], P(('batch', 'head')), may hold values from -6 to 6
- norm1_gain: float32 [2048], replicated, may hold values from 0.5 to 1.5
- qkv_weight: bfloat16 [3, 2048, 2048], P(None, None, 'head'), may hold values from -0.125 to 0.125
- beta_weight: bfloat16 [2048, 16], P(None, 'head'), may hold values from -0.125 to 0.125
- conv_weight: bfloat16 [3, 4, 2048], P(None, None, 'head'), may hold values from -3 to 3
- out_gain: float32 [128], replicated, may hold values from 0.5 to 1.5
- out_weight: bfloat16 [2048, 2048], P('head'), may hold values from -0.125 to 0.125
- norm2_gain: float32 [2048], replicated, may hold values from 0.5 to 1.5
- gate_up_weight: bfloat16 [2, 2048, 5632], P(None, None, 'head'), may hold values from -0.125 to 0.125
- down_weight: bfloat16 [5632, 2048], P('head'), may hold values from -0.078125 to 0.078125
- block_segments: int32 [8, 4], P('batch'), may hold values from 0 to 2, never falling along the last dimension, each value on 1 to 2 neighbouring positions
- cotangent: bfloat16 [2048, 2048], P(('batch', 'head')), may hold values from -6 to 6
Outputs:
- block_out: bfloat16 [2048, 2048], P(('batch', 'head'))
- input_grad: float32 [2048, 2048], P(('batch', 'head'))
- norm1_gain_grad: float32 [2048], replicated
- qkv_grad: float32 [3, 2048, 2048], P(None, None, 'head')
- beta_grad: float32 [2048, 16], P(None, 'head')
- conv_grad: float32 [3, 4, 2048], P(None, None, 'head')
- out_gain_grad: float32 [128], replicated
- out_grad: float32 [2048, 2048], P('head')
- norm2_gain_grad: float32 [2048], replicated
- gate_up_grad: float32 [2, 2048, 5632], P(None, None, 'head')
- down_grad: float32 [5632, 2048], P('head')
Inputs may be any that keep to these rules, and one draw needn't show every extreme that they name: `block_segments`: each row gives, for each block of 64 tokens of one group in order, the number of the sequence it belongs to: three sequences in every group, numbered from 0 and never falling; each covers 1 to 2 blocks and one covers exactly 2.
All inputs are finite; a program needn't handle non-finite values.
Results may differ from a plain program's by a relative error of at most 0.02.
Values may be sent and summed in bfloat16 or wider, within the bound.
No kernel may reach another device: no remote copies, remote signals or barrier semaphores. Data moves between devices by JAX's collectives and lax.ppermute only.
A program may use at most 256 MiB of HBM per device.

v0:
```python
import jax
import jax.numpy as jnp
from jax import lax
from jax.sharding import PartitionSpec as P

highest_precision = lax.Precision.HIGHEST


def rms_norm(values, gain, epsilon):
    return values * lax.rsqrt(jnp.mean(values * values, axis=-1, keepdims=True) + epsilon) * gain


def unit_rows(field):
    return field * lax.rsqrt(jnp.sum(field * field, axis=-1, keepdims=True) + 1e-06)


def conv_masks(token_segments, taps):
    masks = []
    for shift in range(1, taps):
        earlier = jnp.concatenate([jnp.full((shift,), -1, jnp.int32), token_segments[:-shift]])
        masks.append((earlier == token_segments).astype(jnp.float32)[:, None])
    return masks


def short_conv(values, taps, masks):
    result = values * taps[0]
    for shift in range(1, taps.shape[0]):
        moved = jnp.concatenate(
            [jnp.zeros((shift, values.shape[1]), jnp.float32), values[:-shift]], axis=0
        )
        result = result + moved * taps[shift] * masks[shift - 1]
    return result


def block_step(running_state, inputs):
    query_rows, key, value, beta, keep = inputs
    running_state = running_state * keep
    length = key.shape[1]
    strict = jnp.tril(jnp.ones((length, length), jnp.float32), -1)
    inclusive = jnp.tril(jnp.ones((length, length), jnp.float32))
    keyed = (
        jnp.einsum("hck,hdk->hcd", key * beta[:, :, None], key, precision=highest_precision)
        * strict
    )
    power = -keyed
    inverse = jnp.eye(length, dtype=jnp.float32) + power
    for level in range(length.bit_length() - 2):
        power = jnp.einsum("hcd,hde->hce", power, power, precision=highest_precision)
        inverse = inverse + jnp.einsum("hcd,hde->hce", inverse, power, precision=highest_precision)
    weights = inverse * beta[:, None, :]
    weighted_key = jnp.einsum("hcd,hdk->hck", weights, key, precision=highest_precision)
    weighted_value = jnp.einsum("kzw,kwp->kzp", weights, value, precision=highest_precision)
    fresh_values = weighted_value - jnp.einsum(
        "imd,ide->ime", weighted_key, running_state, precision=highest_precision
    )
    score_matrix = (
        jnp.einsum("hck,hdk->hcd", query_rows, key, precision=highest_precision) * inclusive
    )
    output_rows = jnp.einsum(
        "imd,ide->ime", query_rows, running_state, precision=highest_precision
    ) + jnp.einsum("kzw,kwp->kzp", score_matrix, fresh_values, precision=highest_precision)
    running_state = running_state + jnp.einsum(
        "sbi,sbw->siw", key, fresh_values, precision=highest_precision
    )
    return (running_state, output_rows)


def local_mixer(projected, beta_logit, conv_taps, gain, token_segments, keep):
    masks = conv_masks(token_segments, conv_taps.shape[1])
    heads = beta_logit.shape[1]
    length = projected.shape[1]
    width = projected.shape[2] // heads
    blocks = keep.shape[0]
    size = length // blocks
    parts = []
    for which in range(3):
        convolved = jax.nn.silu(short_conv(projected[which], conv_taps[which], masks))
        parts.append(convolved.reshape(length, heads, width))
    query_rows = unit_rows(parts[0]) * width ** (-0.5)
    key = unit_rows(parts[1])
    value = parts[2]
    beta = jax.nn.sigmoid(beta_logit)

    def arrange(field):
        return field.reshape(blocks, size, heads, width).transpose(0, 2, 1, 3)

    beta_blocks = beta.reshape(blocks, size, heads).transpose(0, 2, 1)
    initial = jnp.zeros((heads, width, width), jnp.float32)
    final, outputs = lax.scan(
        jax.checkpoint(block_step),
        initial,
        (arrange(query_rows), arrange(key), arrange(value), beta_blocks, keep),
    )
    outputs = outputs.transpose(0, 2, 1, 3).reshape(length, heads, width)
    return rms_norm(outputs, gain, 1e-05).reshape(length, heads * width)


def norm_rows(values, gain):
    return rms_norm(values, gain, 1e-06)


def per_device(
    hidden_in,
    norm1_gain,
    qkv_weight,
    beta_weight,
    conv_weight,
    out_gain,
    out_weight,
    norm2_gain,
    gate_up_weight,
    down_weight,
    block_segments,
    cotangent,
):
    segments = block_segments[0]
    blocks = segments.shape[0]
    rows_in = hidden_in.astype(jnp.float32)
    normed_one, first_pull = jax.vjp(norm_rows, rows_in, norm1_gain)
    normed_low = normed_one.astype(jnp.bfloat16)
    normed_all = lax.all_gather(normed_low, "head", axis=0, tiled=True)
    length = normed_all.shape[0]
    token_segments = jnp.repeat(segments, length // blocks)
    keep = jnp.concatenate(
        [jnp.zeros((1,), jnp.float32), (segments[1:] == segments[:-1]).astype(jnp.float32)]
    )
    projected = jnp.einsum(
        "td,sde->ste", normed_all, qkv_weight, preferred_element_type=jnp.float32
    )
    beta_logit = jnp.dot(normed_all, beta_weight, preferred_element_type=jnp.float32)

    def mixer(projected_in, beta_in, conv_in, gain_in):
        return local_mixer(projected_in, beta_in, conv_in, gain_in, token_segments, keep)

    mixer_out, mixer_pull = jax.vjp(
        mixer, projected, beta_logit, conv_weight.astype(jnp.float32), out_gain
    )
    mixer_low = mixer_out.astype(jnp.bfloat16)
    piece = mixer_low
    attn_rows = lax.psum_scatter(
        jnp.dot(piece, out_weight, preferred_element_type=jnp.float32).astype(jnp.bfloat16),
        "head",
        scatter_dimension=0,
        tiled=True,
    ).astype(jnp.float32)
    middle = rows_in + attn_rows
    normed_two, second_pull = jax.vjp(norm_rows, middle, norm2_gain)
    second_low = normed_two.astype(jnp.bfloat16)
    second_all = lax.all_gather(second_low, "head", axis=0, tiled=True)
    gate_up = jnp.einsum(
        "td,sdf->stf", second_all, gate_up_weight, preferred_element_type=jnp.float32
    )
    sigmoid_gate = jax.nn.sigmoid(gate_up[0])
    silu_gate = gate_up[0] * sigmoid_gate
    hidden_low = (silu_gate * gate_up[1]).astype(jnp.bfloat16)
    piece = hidden_low
    ffn_rows = lax.psum_scatter(
        jnp.dot(piece, down_weight, preferred_element_type=jnp.float32).astype(jnp.bfloat16),
        "head",
        scatter_dimension=0,
        tiled=True,
    ).astype(jnp.float32)
    block_out = (middle + ffn_rows).astype(jnp.bfloat16)
    cot_all = lax.all_gather(cotangent, "head", axis=0, tiled=True)
    down_grad = jnp.einsum("tf,td->fd", hidden_low, cot_all, preferred_element_type=jnp.float32)
    hidden_grad = jnp.einsum("td,fd->tf", cot_all, down_weight, preferred_element_type=jnp.float32)
    gate_grad = hidden_grad * gate_up[1] * sigmoid_gate * (1.0 + gate_up[0] * (1.0 - sigmoid_gate))
    up_grad = hidden_grad * silu_gate
    gate_up_low = jnp.stack([gate_grad, up_grad]).astype(jnp.bfloat16)
    gate_up_grad = jnp.einsum(
        "td,stf->sdf", second_all, gate_up_low, preferred_element_type=jnp.float32
    )
    piece = gate_up_low
    second_grad = lax.psum_scatter(
        jnp.einsum("stf,sdf->td", piece, gate_up_weight, preferred_element_type=jnp.float32).astype(
            jnp.bfloat16
        ),
        "head",
        scatter_dimension=0,
        tiled=True,
    ).astype(jnp.float32)
    middle_part, norm2_gain_grad = second_pull(second_grad)
    middle_grad = cotangent.astype(jnp.float32) + middle_part
    mixer_grad_all = lax.all_gather(middle_grad.astype(jnp.bfloat16), "head", axis=0, tiled=True)
    out_grad = jnp.einsum(
        "tc,td->cd", mixer_low, mixer_grad_all, preferred_element_type=jnp.float32
    )
    mixer_in_grad = jnp.einsum(
        "td,cd->tc", mixer_grad_all, out_weight, preferred_element_type=jnp.float32
    )
    projected_grad, beta_logit_grad, conv_grad, out_gain_grad = mixer_pull(mixer_in_grad)
    projected_low = projected_grad.astype(jnp.bfloat16)
    beta_low = beta_logit_grad.astype(jnp.bfloat16)
    qkv_grad = jnp.einsum(
        "td,ste->sde", normed_all, projected_low, preferred_element_type=jnp.float32
    )
    beta_grad = jnp.einsum("td,th->dh", normed_all, beta_low, preferred_element_type=jnp.float32)
    piece = projected_low
    first_grad = lax.psum_scatter(
        (
            jnp.einsum("ste,sde->td", piece, qkv_weight, preferred_element_type=jnp.float32)
            + jnp.einsum("th,dh->td", beta_low, beta_weight, preferred_element_type=jnp.float32)
        ).astype(jnp.bfloat16),
        "head",
        scatter_dimension=0,
        tiled=True,
    ).astype(jnp.float32)
    rows_part, norm1_gain_grad = first_pull(first_grad)
    input_grad = middle_grad + rows_part
    norm1_gain_grad, norm2_gain_grad, out_gain_grad = lax.psum(
        (norm1_gain_grad, norm2_gain_grad, out_gain_grad), ("batch", "head")
    )
    qkv_grad, beta_grad, conv_grad, out_grad, gate_up_grad, down_grad = (
        lax.psum(qkv_grad.astype(jnp.bfloat16), "batch").astype(jnp.float32),
        lax.psum(beta_grad.astype(jnp.bfloat16), "batch").astype(jnp.float32),
        lax.psum(conv_grad.astype(jnp.bfloat16), "batch").astype(jnp.float32),
        lax.psum(out_grad.astype(jnp.bfloat16), "batch").astype(jnp.float32),
        lax.psum(gate_up_grad.astype(jnp.bfloat16), "batch").astype(jnp.float32),
        lax.psum(down_grad.astype(jnp.bfloat16), "batch").astype(jnp.float32),
    )
    return (
        block_out,
        input_grad,
        norm1_gain_grad,
        qkv_grad,
        beta_grad,
        conv_grad,
        out_gain_grad,
        out_grad,
        norm2_gain_grad,
        gate_up_grad,
        down_grad,
    )


def solution(mesh):
    placed = (
        P(("batch", "head"), None),
        P(),
        P(None, None, "head"),
        P(None, "head"),
        P(None, None, "head"),
        P(),
        P("head", None),
        P(),
        P(None, None, "head"),
        P("head", None),
        P("batch", None),
        P(("batch", "head"), None),
    )
    return jax.shard_map(
        per_device,
        mesh=mesh,
        in_specs=placed,
        out_specs=(
            P(("batch", "head"), None),
            P(("batch", "head"), None),
            P(),
            P(None, None, "head"),
            P(None, "head"),
            P(None, None, "head"),
            P(),
            P("head", None),
            P(),
            P(None, None, "head"),
            P("head", None),
        ),
        check_vma=False,
    )
```

profile of v0, /device:TPU:0, one launch (start us, length us, event | category | flops | bytes accessed | tf_op | source)
XLA Modules:
  0.0 1058.0 jit_solution(14581154062135182777)
XLA Ops:
  9.7 1.8 fusion.112
  16.7 24.1 %all-gather.5.cloned.1.call-done = bf16[256,2048]{1,0:T(8,128)(2,1)} async-done(((bf16[64,2048]{1,0:T(8,128)(2,1)}), bf16[256,2048]{1,0:T(8,128)(2,1)}) %all-gather.5.cloned.1.call-update) | async-done | bytes 1048592 | tf_op jit(solution)/shard_map/all_gather | solution.py:121
  40.8 4.9 convolution_bitcast_fusion.4
  47.4 1.9 fusion.144
  51.1 2.0 reshape.449
  53.1 2.0 reshape.448
  55.2 2.4 fusion.143
  64.4 2.0 reshape.447
  70.9 2.2 copy_bitcast_fusion
  73.9 54.5 %while.38 = (s32[]{:T(128)}, f32[4,128,128]{2,1,0:T(8,128)S(1)}, f32[4,4,64,128]{3,2,1,0:T(8,128)}, f32[4,4,128,128]{3,2,1,0:T(8,128)}, f32[4]{0:T(128)}, /*inde...) while((s32[]{:T(128)}, f32[4,128,128]{2,1,0:T(8,128)S(1)}, ...), condition=%wide.region_4.5_spmd.clone, body=%wide.region_3.4_spmd.clone.sunk | while | flops 403464192 | bytes 6104994 | solution.py:89
  83.0 2.6 fusion.526
  96.6 2.6 fusion.526
  110.2 2.6 fusion.526
  123.9 2.6 fusion.526
  133.2 1.7 convolution_convert_fusion.2
  135.0 28.0 %reduce-scatter.5.cloned.1.call-done = bf16[64,2048]{1,0:T(8,128)(2,1)} async-done(((bf16[256,2048]{1,0:T(8,128)(2,1)}), bf16[64,2048]{1,0:T(8,128)(2,1)}) %reduce-scatter.5.cloned.1.call-update) | async-done | bytes 262160 | tf_op jit(solution)/shard_map/reduce_scatter | solution.py:140
  164.2 1.8 multiply_convert_fusion.3
  166.8 25.9 %all-gather.7.cloned.1.call-done = bf16[256,2048]{1,0:T(8,128)(2,1)} async-done(((bf16[64,2048]{1,0:T(8,128)(2,1)}), bf16[256,2048]{1,0:T(8,128)(2,1)}) %all-gather.7.cloned.1.call-update) | async-done | bytes 1048592 | tf_op jit(solution)/shard_map/all_gather | solution.py:149
  192.7 9.3 convolution_bitcast_fusion.1
  202.0 18.9 %all-gather.9.cloned.1.call-done = bf16[256,2048]{1,0:T(8,128)(2,1)} async-done(((bf16[64,2048]{1,0:T(8,128)(2,1)}), bf16[256,2048]{1,0:T(8,128)(2,1)}) %all-gather.9.cloned.1.call-update) | async-done | bytes 1048592 | tf_op jit(solution)/shard_map/all_gather | solution.py:164
  220.9 6.9 fusion.107
  228.9 8.5 fusion.96
  237.5 28.0 %reduce-scatter.9.cloned.1.call-done = bf16[64,2048]{1,0:T(8,128)(2,1)} async-done(((bf16[256,2048]{1,0:T(8,128)(2,1)}), bf16[64,2048]{1,0:T(8,128)(2,1)}) %reduce-scatter.9.cloned.1.call-update) | async-done | bytes 262160 | tf_op jit(solution)/shard_map/reduce_scatter | solution.py:174
  265.5 1.8 fusion.114
  267.3 1.9 fusion.142
  269.5 26.4 %all-gather.11.cloned.1.call-done = bf16[256,2048]{1,0:T(8,128)(2,1)} async-done(((bf16[64,2048]{1,0:T(8,128)(2,1)}), bf16[256,2048]{1,0:T(8,128)(2,1)}) %all-gather.11.cloned.1.call-update) | async-done | bytes 1048592 | tf_op jit(solution)/shard_map/all_gather | solution.py:184
  295.9 3.1 multiply_reduce_fusion.2
  304.0 119.5 %while.39 = (s32[]{:T(128)}, f32[4,128,128]{2,1,0:T(8,128)}, f32[4,4,64,128]{3,2,1,0:T(8,128)S(1)}, f32[4,4,64,128]{3,2,1,0:T(8,128)}, f32[4,4,64,128]{3,2,1,0:T...) while((s32[]{:T(128)}, f32[4,128,128]{2,1,0:T(8,128)}, ...), condition=%wide.region_15.16_spmd.clone, body=%wide.region_12.15_spmd.clone.sunk | while | flops 1083678464 | bytes 18188008 | solution.py:89
  331.3 1.9 fusion.643
  361.2 1.9 fusion.643
  391.2 1.9 fusion.643
  421.2 1.9 fusion.643
  439.1 2.9 multiply_reduce_fusion.11
  442.1 5.2 convolution_bitcast_fusion.2
  447.3 1.5 fusion.97
  448.9 5.5 convolution_convert_fusion.3
  454.5 4.2 convolution_convert_fusion
  458.7 6.4 convert_bitcast_fusion.1
  465.2 2.1 convolution_convert_fusion.1
  467.3 4.6 convert_bitcast_fusion.2
  472.2 28.4 %all-reduce.39 = (bf16[2048,4]{0,1:T(4,128)(2,1)S(1)}, bf16[3,4,512]{2,1,0:T(4,128)(2,1)S(1)}) all-reduce(bf16[2048,4]{0,1:T(4,128)(2,1)S(1)} %convolution_convert_fusion.4, bf16[3,4,512]{2,1,0:T(4,128)(2,1)S(1)} %add_convert_fusion.2), channel_id=1, replica_groups=mesh['batch'=8,'head'=4] {'batch'}, use_global_device_ids=true, to_apply=%region_23.24 | all-reduce | flops 14336 | bytes 57344 | tf_op jit(solution)/shard_map/psum | solution.py:215
  503.2 38.7 %all-reduce.38 = (f32[2048]{0:T(1024)}, f32[128]{0:T(128)}, f32[2048]{0:T(1024)}) all-reduce(f32[2048]{0:T(1024)S(1)} %get-tuple-element.622, f32[128]{0:T(128)S(1)} %bitcast_reduce_fusion, f32[2048]{0:T(1024)S(1)} %copy-done.74), channel_id=1, replica_groups=mesh['batch'=8,'head'=4] {'batch','head'}, use_global_device_ids=true, to_apply=%region_21.22 | all-reduce | flops 4224 | bytes 33792 | tf_op jit(solution)/shard_map/psum | solution.py:210
  541.9 2.3 fusion.124
  544.3 469.3 %all-reduce.43.cloned.1.call-done = (bf16[3,2048,512]{1,2,0:T(8,128)(2,1)}, bf16[2,2048,1408]{1,2,0:T(8,128)(2,1)}, bf16[512,2048]{1,0:T(8,128)(2,1)}, bf16[1408,2048]{1,0:T(8,128)(2,1)}) async-done(((bf16[3,2048,512]{1,2,0:T(8,128)(2,1)}, bf16[2,2048,1408]{1,2,0:T(8,128)(2,1)}, bf16[512,2048]{1,0:T(8,128)(2,1)}, bf16[1408,2048]{1,0:T(8,128)(2,1)}), (bf16[3,2048,512]{1,2,0:T(8,128)(2,1)}, ...) | async-done | bytes 25690128 | tf_op jit(solution)/shard_map/psum | solution.py:214
  1013.5 17.0 %copy.272 = f32[2,2048,1408]{2,1,0:T(8,128)} copy(bf16[2,2048,1408]{1,2,0:T(8,128)(2,1)} %get-tuple-element.676) | data formatting | bytes 34603008
  1030.5 9.4 copy.271
  1039.9 8.8 convert_element_type.177
  1048.8 2.5 convert_element_type.172
  (683 shorter events, 207.6 us)
Async XLA Ops:
  7.2 126.1 %copy-start = (bf16[512,2048]{1,0:T(8,128)(2,1)S(1)}, bf16[512,2048]{1,0:T(8,128)(2,1)}, u32[]{:S(2)}) copy-start(bf16[512,2048]{1,0:T(8,128)(2,1)} %param.22) | copy-start | bytes 6291460
  7.2 33.6 %all-gather.5.cloned.1.call-start = ((), (), s32[]{:S(2)}) async-start(), calls=%async_computation.4 | async-start | bytes 1310720 | tf_op jit(solution)/shard_map/all_gather | solution.py:121
  11.5 151.6 %reduce-scatter.5.cloned.1.call-start = ((), (), s32[]{:S(2)}) async-start(), calls=%async_computation.5 | async-start | bytes 1310720 | tf_op jit(solution)/shard_map/reduce_scatter | solution.py:140
  15.7 39.5 %copy-start.100 = (f32[256]{0:T(256)}, f32[256]{0:T(256)S(1)}, u32[]{:S(2)}) copy-start(f32[256]{0:T(256)S(1)} %get-tuple-element.767) | copy-start | bytes 3076
  15.7 39.5 %copy-start.102 = (f32[256]{0:T(256)}, f32[256]{0:T(256)S(1)}, u32[]{:S(2)}) copy-start(f32[256]{0:T(256)S(1)} %get-tuple-element.769) | copy-start | bytes 3076
  15.7 39.5 %copy-start.104 = (f32[256]{0:T(256)}, f32[256]{0:T(256)S(1)}, u32[]{:S(2)}) copy-start(f32[256]{0:T(256)S(1)} %get-tuple-element.768) | copy-start | bytes 3076
  16.6 30.4 %copy-start.76 = (f32[1,1,512]{2,1,0:T(1,128)}, f32[1,1,512]{2,1,0:T(1,128)S(1)}, u32[]{:S(2)}) copy-start(f32[1,1,512]{2,1,0:T(1,128)S(1)} %get-tuple-element.739) | copy-start | bytes 6148
  16.6 30.4 %copy-start.78 = (f32[1,1,512]{2,1,0:T(1,128)}, f32[1,1,512]{2,1,0:T(1,128)S(1)}, u32[]{:S(2)}) copy-start(f32[1,1,512]{2,1,0:T(1,128)S(1)} %get-tuple-element.743) | copy-start | bytes 6148
  16.6 30.4 %copy-start.80 = (f32[1,1,512]{2,1,0:T(1,128)}, f32[1,1,512]{2,1,0:T(1,128)S(1)}, u32[]{:S(2)}) copy-start(f32[1,1,512]{2,1,0:T(1,128)S(1)} %get-tuple-element.746) | copy-start | bytes 6148
  16.6 30.4 %copy-start.82 = (f32[1,1,512]{2,1,0:T(1,128)}, f32[1,1,512]{2,1,0:T(1,128)S(1)}, u32[]{:S(2)}) copy-start(f32[1,1,512]{2,1,0:T(1,128)S(1)} %get-tuple-element.742) | copy-start | bytes 6148
  16.6 30.4 %copy-start.84 = (f32[1,1,512]{2,1,0:T(1,128)}, f32[1,1,512]{2,1,0:T(1,128)S(1)}, u32[]{:S(2)}) copy-start(f32[1,1,512]{2,1,0:T(1,128)S(1)} %get-tuple-element.745) | copy-start | bytes 6148
  16.6 30.4 %copy-start.86 = (f32[1,1,512]{2,1,0:T(1,128)}, f32[1,1,512]{2,1,0:T(1,128)S(1)}, u32[]{:S(2)}) copy-start(f32[1,1,512]{2,1,0:T(1,128)S(1)} %get-tuple-element.744) | copy-start | bytes 6148
  16.6 30.4 %copy-start.88 = (f32[1,1,512]{2,1,0:T(1,128)}, f32[1,1,512]{2,1,0:T(1,128)S(1)}, u32[]{:S(2)}) copy-start(f32[1,1,512]{2,1,0:T(1,128)S(1)} %get-tuple-element.741) | copy-start | bytes 6148
  16.7 30.4 %copy-start.90 = (f32[1,1,512]{2,1,0:T(1,128)}, f32[1,1,512]{2,1,0:T(1,128)S(1)}, u32[]{:S(2)}) copy-start(f32[1,1,512]{2,1,0:T(1,128)S(1)} %get-tuple-element.740) | copy-start | bytes 6148
  16.7 38.5 %copy-start.92 = (f32[1,1,512]{2,1,0:T(1,128)}, f32[1,1,512]{2,1,0:T(1,128)S(1)}, u32[]{:S(2)}) copy-start(f32[1,1,512]{2,1,0:T(1,128)S(1)} %get-tuple-element.747) | copy-start | bytes 6148
  16.7 38.5 %copy-start.94 = (f32[1,1,512]{2,1,0:T(1,128)}, f32[1,1,512]{2,1,0:T(1,128)S(1)}, u32[]{:S(2)}) copy-start(f32[1,1,512]{2,1,0:T(1,128)S(1)} %get-tuple-element.750) | copy-start | bytes 6148
  16.7 38.5 %copy-start.96 = (f32[1,1,512]{2,1,0:T(1,128)}, f32[1,1,512]{2,1,0:T(1,128)S(1)}, u32[]{:S(2)}) copy-start(f32[1,1,512]{2,1,0:T(1,128)S(1)} %get-tuple-element.748) | copy-start | bytes 6148
  16.7 38.5 %copy-start.98 = (f32[1,1,512]{2,1,0:T(1,128)}, f32[1,1,512]{2,1,0:T(1,128)S(1)}, u32[]{:S(2)}) copy-start(f32[1,1,512]{2,1,0:T(1,128)S(1)} %get-tuple-element.749) | copy-start | bytes 6148
  45.9 9.3 copy-start.17
  46.1 9.1 copy-start.23
  60.9 8.9 copy-start.6
  60.9 8.9 copy-start.66
  133.2 29.8 %copy-start.4 = (bf16[64,2048]{1,0:T(8,128)(2,1)S(1)}, bf16[64,2048]{1,0:T(8,128)(2,1)}, u32[]{:S(2)}) copy-start(bf16[64,2048]{1,0:T(8,128)(2,1)} %param.16) | copy-start | bytes 786436
  133.2 30.9 %copy-start.60 = (f32[2048]{0:T(1024)S(1)}, f32[2048]{0:T(1024)}, u32[]{:S(2)}) copy-start(f32[2048]{0:T(1024)} %param.23) | copy-start | bytes 24580
  135.0 57.7 %all-gather.7.cloned.1.call-start = ((), (), s32[]{:S(2)}) async-start(), calls=%async_computation.6 | async-start | bytes 1310720 | tf_op jit(solution)/shard_map/all_gather | solution.py:149
  164.2 103.1 %copy-start.108 = (f32[64]{0:T(128)}, f32[64]{0:T(128)S(1)}, u32[]{:S(2)}) copy-start(f32[64]{0:T(128)S(1)} %fusion.139) | copy-start | bytes 772
  166.0 54.9 %all-gather.9.cloned.1.call-start = ((), (), s32[]{:S(2)}) async-start(), calls=%async_computation.8 | async-start | bytes 1310720 | tf_op jit(solution)/shard_map/all_gather | solution.py:164
  166.6 98.9 %reduce-scatter.9.cloned.1.call-start = ((), (), s32[]{:S(2)}) async-start(), calls=%async_computation.9 | async-start | bytes 1310720 | tf_op jit(solution)/shard_map/reduce_scatter | solution.py:174
  228.9 36.6 %copy-start.8 = (bf16[64,2048]{1,0:T(8,128)(2,1)S(1)}, bf16[64,2048]{1,0:T(8,128)(2,1)}, u32[]{:S(2)}) copy-start(bf16[64,2048]{1,0:T(8,128)(2,1)} %reduce-scatter.5.cloned.1.call-done) | copy-start | bytes 786436
  228.9 38.4 %copy-start.40 = (bf16[64,2048]{1,0:T(8,128)(2,1)S(1)}, bf16[64,2048]{1,0:T(8,128)(2,1)}, u32[]{:S(2)}) copy-start(bf16[64,2048]{1,0:T(8,128)(2,1)} %param.27) | copy-start | bytes 786436
  237.4 31.9 %copy-start.72 = (f32[256,4]{0,1:T(4,128)S(1)}, f32[256,4]{0,1:T(4,128)}, u32[]{:S(2)}) copy-start(f32[256,4]{0,1:T(4,128)} %copy-done.71) | copy-start | bytes 12292
  237.4 58.4 %all-gather.11.cloned.1.call-start = ((), (), s32[]{:S(2)}) async-start(), calls=%async_computation.10 | async-start | bytes 1310720 | tf_op jit(solution)/shard_map/all_gather | solution.py:184
  269.2 232.7 %reduce-scatter.11.cloned.1.call-start = ((), (), s32[]{:S(2)}) async-start(), calls=%async_computation.11 | async-start | bytes 1310720 | tf_op jit(solution)/shard_map/reduce_scatter | solution.py:199
  269.4 30.7 %copy-start.5 = (f32[4,4,64,128]{3,2,1,0:T(8,128)S(1)}, f32[4,4,64,128]{3,2,1,0:T(8,128)}, u32[]{:S(2)}) copy-start(f32[4,4,64,128]{3,2,1,0:T(8,128)} %get-tuple-element.340) | copy-start | bytes 1572868
  269.5 30.7 %copy-start.110 = (f32[128]{0:T(128)S(1)}, f32[128]{0:T(128)}, u32[]{:S(2)}) copy-start(f32[128]{0:T(128)} %param.21) | copy-start | bytes 1540
  448.8 93.1 %reduce-scatter.7.cloned.1.call-start = ((), (), s32[]{:S(2)}) async-start(), calls=%async_computation.7 | async-start | bytes 1310720 | tf_op jit(solution)/shard_map/reduce_scatter | solution.py:157
  454.4 559.1 %all-reduce.43.cloned.1.call-start = ((), (), s32[]{:S(2)}) async-start(), calls=%async_computation.12 | async-start | bytes 51380224 | tf_op jit(solution)/shard_map/psum | solution.py:214
  458.7 6.4 copy-start.37
  471.8 30.1 %copy-start.61 = (f32[2048]{0:T(1024)S(1)}, f32[2048]{0:T(1024)}, u32[]{:S(2)}) copy-start(f32[2048]{0:T(1024)} %param.17) | copy-start | bytes 24580
  471.8 30.1 %copy-start.112 = (f32[64]{0:T(128)S(1)}, f32[64]{0:T(128)}, u32[]{:S(2)}) copy-start(f32[64]{0:T(128)} %copy-done.111) | copy-start | bytes 772
  471.8 31.4 %copy-start.74 = (f32[2048]{0:T(1024)S(1)}, f32[2048]{0:T(1024)}, u32[]{:S(2)}) copy-start(f32[2048]{0:T(1024)} %get-tuple-element.620) | copy-start | bytes 24580
  471.8 70.0 %copy-start.116 = (f32[64]{0:T(128)S(1)}, f32[64]{0:T(128)}, u32[]{:S(2)}) copy-start(f32[64]{0:T(128)} %copy-done.115) | copy-start | bytes 772
  471.8 70.1 %copy-start.9 = (bf16[64,2048]{1,0:T(8,128)(2,1)S(1)}, bf16[64,2048]{1,0:T(8,128)(2,1)}, u32[]{:S(2)}) copy-start(bf16[64,2048]{1,0:T(8,128)(2,1)} %reduce-scatter.5.cloned.1.call-done) | copy-start | bytes 786436
  471.8 70.1 %copy-start.41 = (bf16[64,2048]{1,0:T(8,128)(2,1)S(1)}, bf16[64,2048]{1,0:T(8,128)(2,1)}, u32[]{:S(2)}) copy-start(bf16[64,2048]{1,0:T(8,128)(2,1)} %param.27) | copy-start | bytes 786436
  471.9 70.1 %copy-start.42 = (bf16[64,2048]{1,0:T(8,128)(2,1)S(1)}, bf16[64,2048]{1,0:T(8,128)(2,1)}, u32[]{:S(2)}) copy-start(bf16[64,2048]{1,0:T(8,128)(2,1)} %reduce-scatter.9.cloned.1.call-done) | copy-start | bytes 786436
  471.9 70.1 %copy-start.109 = (f32[64]{0:T(128)S(1)}, f32[64]{0:T(128)}, u32[]{:S(2)}) copy-start(f32[64]{0:T(128)} %copy-done.108) | copy-start | bytes 772
  471.9 70.1 %copy-start.114 = (f32[64]{0:T(128)S(1)}, f32[64]{0:T(128)}, u32[]{:S(2)}) copy-start(f32[64]{0:T(128)} %copy-done.113) | copy-start | bytes 772
  1039.9 8.8 copy-start.43
  (78 other events, 192.4 us)
Sparse Core Ops, SparseCore 0:
  11.6 29.2 all-gather.4
  135.1 27.9 reduce-scatter.4
  166.1 26.4 all-gather.6
  194.4 26.4 all-gather.8
  237.5 27.9 reduce-scatter.8
  269.3 26.4 all-gather.10
  448.9 27.9 reduce-scatter.10
  479.8 27.9 reduce-scatter.6
  511.8 501.6 all-reduce.42
where the time goes:
time: 1070 us; the launch traced here: 1060 us
  waiting for transfers between devices  621 us (58%)
  matrix products  200 us (19%)
  local copies, waits for them, and re-layouts  85.4 us (8%)
  blocking collectives  67 us (6%)
  other arithmetic  65.9 us (6%)
  between operations  15.5 us (1%)
    psum x1, waiting for transfers between devices, per_device(): lax.psum(qkv_grad.astype(jnp.bfloat16), 'batch').astype(jnp.float32)  469 us
    psum x1, blocking collectives, per_device(): lax.psum((norm1_gain_grad, norm2_gain_grad, out_gain_grad), ('batch', 'he...  38.7 us
    unnamed x237, local copies, waits for them, and re-layouts  34.6 us
    psum x1, blocking collectives, per_device(): lax.psum(beta_grad.astype(jnp.bfloat16), 'batch').astype(jnp.float32)  28.4 us
    reduce_scatter x1, waiting for transfers between devices, per_device(): lax.psum_scatter(jnp.einsum('stf,sdf->td', piece, gate_up_weight, preferr...  28 us
    reduce_scatter x1, waiting for transfers between devices, per_device(): lax.psum_scatter(jnp.dot(piece, out_weight, preferred_element_type=jnp.fl...  28 us
    all_gather x1, waiting for transfers between devices, per_device(): lax.all_gather(middle_grad.astype(jnp.bfloat16), 'head', axis=0, tiled=True)  26.4 us
    all_gather x1, waiting for transfers between devices, per_device(): second_all = lax.all_gather(second_low, 'head', axis=0, tiled=True)  25.9 us
  transfers between devices with their start and end apart: 9, of which 7 were waited for; matrix products, arithmetic and copies ran while one was open for 4% of the time, Pallas kernels for 0%

commit v1 on v0

--- a/solution.py
+++ b/solution.py
@@ -211,7 +211,7 @@
         (norm1_gain_grad, norm2_gain_grad, out_gain_grad), ("batch", "head")
     )
     qkv_grad, beta_grad, conv_grad, out_grad, gate_up_grad, down_grad = (
-        lax.psum(qkv_grad.astype(jnp.bfloat16), "batch").astype(jnp.float32),
+        jnp.sum(lax.all_gather(qkv_grad.astype(jnp.bfloat16), "batch"), axis=0).astype(jnp.float32),
         lax.psum(beta_grad.astype(jnp.bfloat16), "batch").astype(jnp.float32),
         lax.psum(conv_grad.astype(jnp.bfloat16), "batch").astype(jnp.float32),
         lax.psum(out_grad.astype(jnp.bfloat16), "batch").astype(jnp.float32),

time: 1070 us -> 1360 us (1.27)
  waiting for transfers between devices: 621 us -> 888 us
  local copies, waits for them, and re-layouts: 85.4 us -> 101 us
  other arithmetic: 65.9 us -> 79.6 us
    all_gather x0 -> x1, waiting for transfers between devices: none -> 397 us  [per_device(): lax.all_gather(qkv_grad.astype(jnp.bfloat16), 'batch')]
    psum x1, waiting for transfers between devices: 469 us -> 339 us  [per_device(): lax.psum(gate_up_grad.astype(jnp.bfloat16), 'batch').astype(jnp.float32)]
    reduce_sum x0 -> x1, other arithmetic: none -> 20.1 us  [per_device(): jnp.sum(lax.all_gather(qkv_grad.astype(jnp.bfloat16), 'batch'), axis=0)]
    unnamed x237 -> x208, local copies, waits for them, and re-layouts: 34.6 us -> 47.1 us
  transfers between devices with their start and end apart: 9 -> 10, of which waited for: 7 -> 8; matrix products, arithmetic and copies ran while one was open for 4% -> 6% of each run, Pallas kernels for 0% -> 0%
where the time goes in v1:
time: 1360 us; the launch traced here: 1350 us
  waiting for transfers between devices  888 us (65%)
  matrix products  197 us (14%)
  local copies, waits for them, and re-layouts  101 us (7%)
  other arithmetic  79.6 us (6%)
  blocking collectives  67.1 us (5%)
  between operations  15.8 us (1%)
    all_gather x1, waiting for transfers between devices, per_device(): lax.all_gather(qkv_grad.astype(jnp.bfloat16), 'batch')  397 us
    psum x1, waiting for transfers between devices, per_device(): lax.psum(gate_up_grad.astype(jnp.bfloat16), 'batch').astype(jnp.float32)  339 us
    unnamed x208, local copies, waits for them, and re-layouts  47.1 us
    psum x1, blocking collectives, per_device(): lax.psum((norm1_gain_grad, norm2_gain_grad, out_gain_grad), ('batch', 'he...  38.7 us
    psum x1, blocking collectives, per_device(): lax.psum(beta_grad.astype(jnp.bfloat16), 'batch').astype(jnp.float32)  28.4 us
    reduce_scatter x1, waiting for transfers between devices, per_device(): lax.psum_scatter(jnp.einsum('stf,sdf->td', piece, gate_up_weight, preferr...  28 us
    reduce_scatter x1, waiting for transfers between devices, per_device(): lax.psum_scatter(jnp.dot(piece, out_weight, preferred_element_type=jnp.fl...  28 us
  transfers between devices with their start and end apart: 10, of which 8 were waited for; matrix products, arithmetic and copies ran while one was open for 6% of the time, Pallas kernels for 0%

profile of v1, /device:TPU:0, one launch (start us, length us, event | category | flops | bytes accessed | tf_op | source)
XLA Modules:
  0.0 1351.5 jit_solution(6283495877814860698)
XLA Ops:
  16.5 24.2 %all-gather.7.cloned.1.call-done = bf16[256,2048]{1,0:T(8,128)(2,1)} async-done(((bf16[64,2048]{1,0:T(8,128)(2,1)}), bf16[256,2048]{1,0:T(8,128)(2,1)}) %all-gather.7.cloned.1.call-update) | async-done | bytes 1048592 | tf_op jit(solution)/shard_map/all_gather | solution.py:121
  40.7 4.9 convolution_bitcast_fusion.4
  51.3 2.0 reshape.445
  53.3 2.0 reshape.444
  55.5 3.8 fusion.144
  71.4 2.0 copy_bitcast_fusion
  73.5 46.5 %while.38 = (s32[]{:T(128)}, f32[4,128,128]{2,1,0:T(8,128)S(1)}, f32[4,4,64,128]{3,2,1,0:T(8,128)S(1)}, f32[4,4,128,128]{3,2,1,0:T(8,128)}, f32[4]{0:T(128)S(1)}...) while((s32[]{:T(128)}, f32[4,128,128]{2,1,0:T(8,128)S(1)}, ...), condition=%wide.region_4.5_spmd.clone, body=%wide.region_3.4_spmd.clone.sunk | while | flops 403464192 | bytes 6104497 | solution.py:89
  81.2 1.9 fusion.526
  92.9 1.9 fusion.526
  116.1 1.9 fusion.526
  124.5 28.0 %reduce-scatter.5.cloned.1.call-done = bf16[64,2048]{1,0:T(8,128)(2,1)} async-done(((bf16[256,2048]{1,0:T(8,128)(2,1)}), bf16[64,2048]{1,0:T(8,128)(2,1)}) %reduce-scatter.5.cloned.1.call-update) | async-done | bytes 262160 | tf_op jit(solution)/shard_map/reduce_scatter | solution.py:140
  156.3 25.9 %all-gather.9.cloned.1.call-done = bf16[256,2048]{1,0:T(8,128)(2,1)} async-done(((bf16[64,2048]{1,0:T(8,128)(2,1)}), bf16[256,2048]{1,0:T(8,128)(2,1)}) %all-gather.9.cloned.1.call-update) | async-done | bytes 1048592 | tf_op jit(solution)/shard_map/all_gather | solution.py:149
  182.1 9.3 convolution_bitcast_fusion.1
  191.5 18.9 %all-gather.11.cloned.1.call-done = bf16[256,2048]{1,0:T(8,128)(2,1)} async-done(((bf16[64,2048]{1,0:T(8,128)(2,1)}), bf16[256,2048]{1,0:T(8,128)(2,1)}) %all-gather.11.cloned.1.call-update) | async-done | bytes 1048592 | tf_op jit(solution)/shard_map/all_gather | solution.py:164
  210.4 6.9 fusion.107
  218.4 8.4 fusion.96
  226.9 28.0 %reduce-scatter.9.cloned.1.call-done = bf16[64,2048]{1,0:T(8,128)(2,1)} async-done(((bf16[256,2048]{1,0:T(8,128)(2,1)}), bf16[64,2048]{1,0:T(8,128)(2,1)}) %reduce-scatter.9.cloned.1.call-update) | async-done | bytes 262160 | tf_op jit(solution)/shard_map/reduce_scatter | solution.py:174
  256.8 2.0 fusion.142
  259.7 25.8 %all-gather.13.cloned.1.call-done = bf16[256,2048]{1,0:T(8,128)(2,1)} async-done(((bf16[64,2048]{1,0:T(8,128)(2,1)}), bf16[256,2048]{1,0:T(8,128)(2,1)}) %all-gather.13.cloned.1.call-update) | async-done | bytes 1048592 | tf_op jit(solution)/shard_map/all_gather | solution.py:184
  285.5 3.6 multiply_reduce_fusion.2
  294.0 116.6 %while.39 = (s32[]{:T(128)}, f32[4,128,128]{2,1,0:T(8,128)}, f32[4,4,64,128]{3,2,1,0:T(8,128)}, f32[4,4,64,128]{3,2,1,0:T(8,128)S(1)}, f32[4,4,64,128]{3,2,1,0:T...) while((s32[]{:T(128)}, f32[4,128,128]{2,1,0:T(8,128)}, ...), condition=%wide.region_15.16_spmd.clone, body=%wide.region_12.15_spmd.clone.sunk | while | flops 1083678464 | bytes 22383908 | solution.py:89
  309.3 1.9 fusion.646
  311.8 2.0 fusion.643
  338.5 1.9 fusion.646
  341.0 2.0 fusion.643
  367.7 1.9 fusion.646
  370.2 2.0 fusion.643
  396.9 1.9 fusion.646
  399.5 2.0 fusion.643
  410.6 2.2 copy.261
  419.1 3.1 multiply_reduce_fusion.14
  431.0 5.7 convolution_convert_fusion.3
  436.8 5.7 convolution_convert_fusion
  442.5 6.4 convert_bitcast_fusion.1
  448.9 2.1 convolution_convert_fusion.1
  452.3 4.5 convert_bitcast_fusion.2
  456.9 8.6 copy.274
  465.9 28.4 %all-reduce.39 = (bf16[2048,4]{0,1:T(4,128)(2,1)S(1)}, bf16[3,4,512]{2,1,0:T(4,128)(2,1)S(1)}) all-reduce(bf16[2048,4]{0,1:T(4,128)(2,1)S(1)} %convolution_convert_fusion.4, bf16[3,4,512]{2,1,0:T(4,128)(2,1)S(1)} %add_convert_fusion.2), channel_id=1, replica_groups=mesh['batch'=8,'head'=4] {'batch'}, use_global_device_ids=true, to_apply=%region_23.24 | all-reduce | flops 14336 | bytes 57344 | tf_op jit(solution)/shard_map/psum | solution.py:215
  496.9 38.7 %all-reduce.38 = (f32[2048]{0:T(1024)}, f32[128]{0:T(128)}, f32[2048]{0:T(1024)}) all-reduce(f32[2048]{0:T(1024)S(1)} %get-tuple-element.622, f32[128]{0:T(128)S(1)} %bitcast_reduce_fusion, f32[2048]{0:T(1024)S(1)} %copy-done.58), channel_id=1, replica_groups=mesh['batch'=8,'head'=4] {'batch','head'}, use_global_device_ids=true, to_apply=%region_21.22 | all-reduce | flops 4224 | bytes 33792 | tf_op jit(solution)/shard_map/psum | solution.py:210
  535.7 2.3 fusion.124
  538.0 339.1 %all-reduce.43.cloned.1.call-done = (bf16[2,2048,1408]{1,2,0:T(8,128)(2,1)}, bf16[512,2048]{1,0:T(8,128)(2,1)}, bf16[1408,2048]{1,0:T(8,128)(2,1)}) async-done(((bf16[2,2048,1408]{1,2,0:T(8,128)(2,1)}, bf16[512,2048]{1,0:T(8,128)(2,1)}, bf16[1408,2048]{1,0:T(8,128)(2,1)}), (bf16[2,2048,1408]{1,2,0:T(8,128)(2,1)}, bf16[512,2048]{1,0:T(8,128)(2,1)}, ...) | async-done | bytes 19398672 | tf_op jit(solution)/shard_map/psum | solution.py:218
  877.0 4.1 convert_element_type.174
  881.2 17.9 %copy.278 = f32[2,2048,1408]{2,1,0:T(8,128)} copy(bf16[2,2048,1408]{1,2,0:T(8,128)(2,1)} %get-tuple-element.675) | data formatting | bytes 34603008
  899.1 9.7 convert_element_type.179
  908.8 397.3 %all-gather.15.cloned.1.call-done = bf16[24,2048,512]{2,1,0:T(8,128)(2,1)} async-done(((bf16[3,2048,512]{2,1,0:T(8,128)(2,1)}), bf16[24,2048,512]{2,1,0:T(8,128)(2,1)}) %all-gather.15.cloned.1.call-update) | async-done | bytes 50331664 | tf_op jit(solution)/shard_map/all_gather | solution.py:214
  1306.1 20.1 %reduce_sum.306 = bf16[3,2048,512]{2,1,0:T(8,128)(2,1)} reduce(bf16[8,3,2048,512]{3,2,1,0:T(8,128)(2,1)} %bitcast.720, bf16[]{:T(256)} %constant.146.clone.1), dimensions={0}, to_apply=%region_22.23 | reduce | flops 22020096 | bytes 56623104 | tf_op jit(solution)/shard_map/reduce_sum | solution.py:214
  1326.2 8.8 copy.301
  1334.9 9.6 copy.277
  (676 shorter events, 201.7 us)
Async XLA Ops:
  7.2 115.5 %copy-start = (bf16[512,2048]{1,0:T(8,128)(2,1)S(1)}, bf16[512,2048]{1,0:T(8,128)(2,1)}, u32[]{:S(2)}) copy-start(bf16[512,2048]{1,0:T(8,128)(2,1)} %param.22) | copy-start | bytes 6291460
  7.2 33.6 %all-gather.7.cloned.1.call-start = ((), (), s32[]{:S(2)}) async-start(), calls=%async_computation.4 | async-start | bytes 1310720 | tf_op jit(solution)/shard_map/all_gather | solution.py:121
  11.4 141.1 %reduce-scatter.5.cloned.1.call-start = ((), (), s32[]{:S(2)}) async-start(), calls=%async_computation.5 | async-start | bytes 1310720 | tf_op jit(solution)/shard_map/reduce_scatter | solution.py:140
  15.5 39.9 %copy-start.84 = (f32[256]{0:T(256)}, f32[256]{0:T(256)S(1)}, u32[]{:S(2)}) copy-start(f32[256]{0:T(256)S(1)} %get-tuple-element.766) | copy-start | bytes 3076
  15.5 39.9 %copy-start.86 = (f32[256]{0:T(256)}, f32[256]{0:T(256)S(1)}, u32[]{:S(2)}) copy-start(f32[256]{0:T(256)S(1)} %get-tuple-element.768) | copy-start | bytes 3076
  15.5 39.9 %copy-start.88 = (f32[256]{0:T(256)}, f32[256]{0:T(256)S(1)}, u32[]{:S(2)}) copy-start(f32[256]{0:T(256)S(1)} %get-tuple-element.767) | copy-start | bytes 3076
  16.4 31.9 %copy-start.76 = (f32[1,1,512]{2,1,0:T(1,128)}, f32[1,1,512]{2,1,0:T(1,128)S(1)}, u32[]{:S(2)}) copy-start(f32[1,1,512]{2,1,0:T(1,128)S(1)} %get-tuple-element.746) | copy-start | bytes 6148
  16.4 31.9 %copy-start.78 = (f32[1,1,512]{2,1,0:T(1,128)}, f32[1,1,512]{2,1,0:T(1,128)S(1)}, u32[]{:S(2)}) copy-start(f32[1,1,512]{2,1,0:T(1,128)S(1)} %get-tuple-element.749) | copy-start | bytes 6148
  16.4 31.9 %copy-start.80 = (f32[1,1,512]{2,1,0:T(1,128)}, f32[1,1,512]{2,1,0:T(1,128)S(1)}, u32[]{:S(2)}) copy-start(f32[1,1,512]{2,1,0:T(1,128)S(1)} %get-tuple-element.748) | copy-start | bytes 6148
  16.4 31.9 %copy-start.82 = (f32[1,1,512]{2,1,0:T(1,128)}, f32[1,1,512]{2,1,0:T(1,128)S(1)}, u32[]{:S(2)}) copy-start(f32[1,1,512]{2,1,0:T(1,128)S(1)} %get-tuple-element.747) | copy-start | bytes 6148
  16.5 38.9 %copy-start.60 = (f32[1,1,512]{2,1,0:T(1,128)}, f32[1,1,512]{2,1,0:T(1,128)S(1)}, u32[]{:S(2)}) copy-start(f32[1,1,512]{2,1,0:T(1,128)S(1)} %get-tuple-element.738) | copy-start | bytes 6148
  16.5 38.9 %copy-start.62 = (f32[1,1,512]{2,1,0:T(1,128)}, f32[1,1,512]{2,1,0:T(1,128)S(1)}, u32[]{:S(2)}) copy-start(f32[1,1,512]{2,1,0:T(1,128)S(1)} %get-tuple-element.742) | copy-start | bytes 6148
  16.5 38.9 %copy-start.64 = (f32[1,1,512]{2,1,0:T(1,128)}, f32[1,1,512]{2,1,0:T(1,128)S(1)}, u32[]{:S(2)}) copy-start(f32[1,1,512]{2,1,0:T(1,128)S(1)} %get-tuple-element.741) | copy-start | bytes 6148
  16.5 38.9 %copy-start.66 = (f32[1,1,512]{2,1,0:T(1,128)}, f32[1,1,512]{2,1,0:T(1,128)S(1)}, u32[]{:S(2)}) copy-start(f32[1,1,512]{2,1,0:T(1,128)S(1)} %get-tuple-element.745) | copy-start | bytes 6148
  16.5 38.9 %copy-start.68 = (f32[1,1,512]{2,1,0:T(1,128)}, f32[1,1,512]{2,1,0:T(1,128)S(1)}, u32[]{:S(2)}) copy-start(f32[1,1,512]{2,1,0:T(1,128)S(1)} %get-tuple-element.744) | copy-start | bytes 6148
  16.5 38.9 %copy-start.70 = (f32[1,1,512]{2,1,0:T(1,128)}, f32[1,1,512]{2,1,0:T(1,128)S(1)}, u32[]{:S(2)}) copy-start(f32[1,1,512]{2,1,0:T(1,128)S(1)} %get-tuple-element.743) | copy-start | bytes 6148
  16.5 38.9 %copy-start.72 = (f32[1,1,512]{2,1,0:T(1,128)}, f32[1,1,512]{2,1,0:T(1,128)S(1)}, u32[]{:S(2)}) copy-start(f32[1,1,512]{2,1,0:T(1,128)S(1)} %get-tuple-element.739) | copy-start | bytes 6148
  16.5 38.9 %copy-start.74 = (f32[1,1,512]{2,1,0:T(1,128)}, f32[1,1,512]{2,1,0:T(1,128)S(1)}, u32[]{:S(2)}) copy-start(f32[1,1,512]{2,1,0:T(1,128)S(1)} %get-tuple-element.740) | copy-start | bytes 6148
  47.0 8.4 copy-start.10
  47.0 8.4 copy-start.12
  63.7 6.7 copy-start.35
  64.7 6.7 copy-start.37
  64.8 8.7 copy-start.54
  64.8 8.7 copy-start.56
  122.7 29.8 %copy-start.4 = (bf16[64,2048]{1,0:T(8,128)(2,1)S(1)}, bf16[64,2048]{1,0:T(8,128)(2,1)}, u32[]{:S(2)}) copy-start(bf16[64,2048]{1,0:T(8,128)(2,1)} %param.16) | copy-start | bytes 786436
  122.7 31.0 %copy-start.45 = (f32[2048]{0:T(1024)S(1)}, f32[2048]{0:T(1024)}, u32[]{:S(2)}) copy-start(f32[2048]{0:T(1024)} %param.23) | copy-start | bytes 24580
  124.4 57.7 %all-gather.9.cloned.1.call-start = ((), (), s32[]{:S(2)}) async-start(), calls=%async_computation.6 | async-start | bytes 1310720 | tf_op jit(solution)/shard_map/all_gather | solution.py:149
  153.7 103.1 %copy-start.92 = (f32[64]{0:T(128)}, f32[64]{0:T(128)S(1)}, u32[]{:S(2)}) copy-start(f32[64]{0:T(128)S(1)} %fusion.139) | copy-start | bytes 772
  155.5 54.9 %all-gather.11.cloned.1.call-start = ((), (), s32[]{:S(2)}) async-start(), calls=%async_computation.8 | async-start | bytes 1310720 | tf_op jit(solution)/shard_map/all_gather | solution.py:164
  156.1 98.8 %reduce-scatter.9.cloned.1.call-start = ((), (), s32[]{:S(2)}) async-start(), calls=%async_computation.9 | async-start | bytes 1310720 | tf_op jit(solution)/shard_map/reduce_scatter | solution.py:174
  226.8 58.7 %all-gather.13.cloned.1.call-start = ((), (), s32[]{:S(2)}) async-start(), calls=%async_computation.10 | async-start | bytes 1310720 | tf_op jit(solution)/shard_map/all_gather | solution.py:184
  258.8 236.8 %reduce-scatter.11.cloned.1.call-start = ((), (), s32[]{:S(2)}) async-start(), calls=%async_computation.11 | async-start | bytes 1310720 | tf_op jit(solution)/shard_map/reduce_scatter | solution.py:199
  430.9 104.7 %reduce-scatter.7.cloned.1.call-start = ((), (), s32[]{:S(2)}) async-start(), calls=%async_computation.7 | async-start | bytes 1310720 | tf_op jit(solution)/shard_map/reduce_scatter | solution.py:157
  436.7 440.3 %all-reduce.43.cloned.1.call-start = ((), (), s32[]{:S(2)}) async-start(), calls=%async_computation.13 | async-start | bytes 38797312 | tf_op jit(solution)/shard_map/psum | solution.py:218
  442.5 6.4 copy-start.26
  442.5 6.4 copy-start.28
  451.0 855.1 %all-gather.15.cloned.1.call-start = ((), (), s32[]{:S(2)}) async-start(), calls=%async_computation.12 | async-start | bytes 56623104 | tf_op jit(solution)/shard_map/all_gather | solution.py:214
  465.5 30.0 %copy-start.90 = (f32[512]{0:T(512)S(1)}, f32[512]{0:T(512)}, u32[]{:S(2)}) copy-start(f32[512]{0:T(512)} %get-tuple-element.769) | copy-start | bytes 6148
  465.5 30.1 %copy-start.46 = (f32[2048]{0:T(1024)S(1)}, f32[2048]{0:T(1024)}, u32[]{:S(2)}) copy-start(f32[2048]{0:T(1024)} %param.17) | copy-start | bytes 24580
  465.5 30.1 %copy-start.96 = (f32[64]{0:T(128)S(1)}, f32[64]{0:T(128)}, u32[]{:S(2)}) copy-start(f32[64]{0:T(128)} %copy-done.95) | copy-start | bytes 772
  465.5 31.4 %copy-start.58 = (f32[2048]{0:T(1024)S(1)}, f32[2048]{0:T(1024)}, u32[]{:S(2)}) copy-start(f32[2048]{0:T(1024)} %get-tuple-element.620) | copy-start | bytes 24580
  465.5 70.1 %copy-start.100 = (f32[64]{0:T(128)S(1)}, f32[64]{0:T(128)}, u32[]{:S(2)}) copy-start(f32[64]{0:T(128)} %copy-done.99) | copy-start | bytes 772
  465.5 70.1 %copy-start.6 = (bf16[64,2048]{1,0:T(8,128)(2,1)S(1)}, bf16[64,2048]{1,0:T(8,128)(2,1)}, u32[]{:S(2)}) copy-start(bf16[64,2048]{1,0:T(8,128)(2,1)} %reduce-scatter.5.cloned.1.call-done) | copy-start | bytes 786436
  465.5 70.1 %copy-start.31 = (bf16[64,2048]{1,0:T(8,128)(2,1)S(1)}, bf16[64,2048]{1,0:T(8,128)(2,1)}, u32[]{:S(2)}) copy-start(bf16[64,2048]{1,0:T(8,128)(2,1)} %param.27) | copy-start | bytes 786436
  465.5 70.1 %copy-start.32 = (bf16[64,2048]{1,0:T(8,128)(2,1)S(1)}, bf16[64,2048]{1,0:T(8,128)(2,1)}, u32[]{:S(2)}) copy-start(bf16[64,2048]{1,0:T(8,128)(2,1)} %reduce-scatter.9.cloned.1.call-done) | copy-start | bytes 786436
  465.6 70.1 %copy-start.93 = (f32[64]{0:T(128)S(1)}, f32[64]{0:T(128)}, u32[]{:S(2)}) copy-start(f32[64]{0:T(128)} %copy-done.92) | copy-start | bytes 772
  465.6 70.1 %copy-start.98 = (f32[64]{0:T(128)S(1)}, f32[64]{0:T(128)}, u32[]{:S(2)}) copy-start(f32[64]{0:T(128)} %copy-done.97) | copy-start | bytes 772
  1334.9 9.6 copy-start.1
  (72 other events, 171.2 us)
Sparse Core Ops, SparseCore 0:
  11.5 29.2 all-gather.6
  124.5 27.9 reduce-scatter.4
  155.6 26.4 all-gather.8
  183.8 26.4 all-gather.10
  226.9 27.9 reduce-scatter.8
  258.9 26.4 all-gather.12
  431.0 27.9 reduce-scatter.10
  461.9 27.9 reduce-scatter.6
  493.8 383.1 all-reduce.42
  878.5 427.4 all-gather.14
